TPU v7x, 32 devices: a whole 2x2x4 slice. The times are simulated.
32 devices in a mesh: tm: 4 (over z), row: 8 (over y, x, core).
Axes of the slice: x: 2, y: 2, z: 4, core: 2. Of those that a mesh axis runs over, the one named last changes fastest.
Arguments:
- features: bfloat16 [256, 8, 37, 256], P('row', 'tm'), may hold values from -8 to 8
- frame_mask: int32 [256], P('row'), may hold values from 0 to 1, as said below
- norm_gain: float32 [256], replicated, may hold values from 0.25 to 1.75
- input_weight: bfloat16 [256, 768], replicated, may hold values from -12 to 12
- output_weight: bfloat16 [256, 256], replicated, may hold values from -0.375 to 0.375
- first_kernel: bfloat16 [9, 256, 128], replicated, may hold values from -0.125 to 0.125
- first_bias: float32 [128], replicated, may hold values from -3 to 3
- second_kernel: bfloat16 [9, 128, 32], replicated, may hold values from -0.1875 to 0.1875
- second_bias: float32 [32], replicated, may hold values from -3 to 3
Outputs:
- depth_head: bfloat16 [256, 8, 1184], P('row', 'tm')
Inputs may be any that keep to these rules, and one draw needn't show every extreme that they name: frame_mask is 1 on frames 0 to n - 1 and 0 on the rest, for some n with 192 < n < 256.
All inputs are finite; a program needn't handle non-finite values.
Results may differ from a plain program's by a relative error of at most 0.0057.
Values may be sent and summed in bfloat16 or wider, within the bound.
A program may use at most 128 MiB of HBM per device.

v0:
```python
import math

import jax
import jax.numpy as jnp
from jax import lax
from jax.sharding import PartitionSpec as P

HEADS = 8
WIN = 32


epsilon = 1e-05


def shifted(block, axis, distance):
    devices = range(lax.axis_size(axis))
    route = [(i - distance, i) for i in devices if i - distance in devices]
    return lax.ppermute(block, axis, route)


def extended_2(cells, sides, width):
    for axis, dim in sides:
        count = lax.axis_size(axis)
        ends = count - 1
        head = lax.slice_in_dim(cells, 0, width, axis=dim)
        tail = lax.slice_in_dim(cells, cells.shape[dim] - width, cells.shape[dim], axis=dim)
        cells = jnp.concatenate(
            [
                lax.ppermute(tail, axis, [(i, (i + 1) % count) for i in range(ends)]),
                cells,
                lax.ppermute(head, axis, [((i + 1) % count, i) for i in range(ends)]),
            ],
            axis=dim,
        )
    return cells


def layer_norm(field, norm_gain):
    widened = field.astype(jnp.float32)
    average = jnp.mean(widened, axis=-1, keepdims=True)
    centered = widened - average
    variance = jnp.mean(centered * centered, axis=-1, keepdims=True)
    return (centered * lax.rsqrt(variance + epsilon) * norm_gain).astype(jnp.bfloat16)


def convolve(field, kernel, bias):
    padded = jnp.pad(field, ((0, 0), (0, 0), (1, 1), (0, 0)))
    height = field.shape[1] - 2
    width = field.shape[2]
    running = jnp.zeros((field.shape[0], height, width, kernel.shape[2]), jnp.float32)
    for tap_row in range(3):
        for tap_col in range(3):
            window = padded[:, tap_row : tap_row + height, tap_col : tap_col + width]
            running = running + jnp.einsum(
                "frwc,cd->frwd",
                window,
                kernel[3 * tap_row + tap_col],
                preferred_element_type=jnp.float32,
            )
    return jnp.maximum(running + bias, 0.0)


def attend(query, key_value, frame_mask, tail_pairs, tail_mask):
    frames, places, channels = query.shape
    head_size = channels // HEADS
    block_count = frames // WIN
    extended = jnp.concatenate(
        [tail_pairs, key_value, jnp.zeros((1, places, 2 * channels), jnp.bfloat16)], axis=0
    )
    mask_ext = jnp.concatenate([tail_mask, frame_mask, jnp.zeros((1,), jnp.int32)])
    blocks = extended.reshape(block_count + 1, WIN, places, 2 * channels)
    mask_blocks = mask_ext.reshape(block_count + 1, WIN)
    query_blocks = query.reshape(block_count, WIN, places, HEADS, head_size)
    query_pos = jnp.arange(WIN, dtype=jnp.int32)[:, None]
    key_pos = jnp.arange(2 * WIN, dtype=jnp.int32)[None, :]
    inside = (key_pos >= query_pos) & (key_pos <= query_pos + WIN - 1)
    itself = key_pos == query_pos + WIN - 1

    def one_block(block_id):
        paired = jnp.concatenate([blocks[block_id], blocks[block_id + 1]], axis=0)
        mask_pair = jnp.concatenate([mask_blocks[block_id], mask_blocks[block_id + 1]])
        key_part = paired[..., :channels].reshape(2 * WIN, places, HEADS, head_size)
        value_part = paired[..., channels:].reshape(2 * WIN, places, HEADS, head_size)
        scores = jnp.einsum(
            "iphd,jphd->phij", query_blocks[block_id], key_part, preferred_element_type=jnp.float32
        ) * (1.0 / math.sqrt(head_size))
        allowed = inside & ((mask_pair[None, :] == 1) | itself)
        scores = jnp.where(allowed[None, None], scores, -1e30)
        largest = jnp.max(scores, axis=-1, keepdims=True)
        powers = jnp.exp(scores - largest)
        weights = (powers / jnp.sum(powers, axis=-1, keepdims=True)).astype(jnp.bfloat16)
        return jnp.einsum(
            "phij,jphd->iphd", weights, value_part, preferred_element_type=jnp.float32
        ).astype(jnp.bfloat16)

    gathered = lax.map(one_block, jnp.arange(block_count, dtype=jnp.int32))
    return gathered.reshape(frames, places, channels)


def body(
    features,
    frame_mask,
    norm_gain,
    input_weight,
    output_weight,
    first_kernel,
    first_bias,
    second_kernel,
    second_bias,
):
    frames, rows, width, channels = features.shape
    places = rows * width
    reach = WIN - 1
    flat = features.reshape(frames, places, channels)
    normed = layer_norm(flat, norm_gain)
    projected = jnp.einsum(
        "fpc,cd->fpd", normed, input_weight, preferred_element_type=jnp.float32
    ).astype(jnp.bfloat16)
    query = projected[:, :, :channels]
    key_value = projected[:, :, channels:]
    tail_normed, tail_mask = shifted(
        (normed[frames - reach :], frame_mask[frames - reach :]), "row", 1
    )
    tail_pairs = jnp.einsum(
        "fpc,cd->fpd", tail_normed, input_weight[:, channels:], preferred_element_type=jnp.float32
    ).astype(jnp.bfloat16)
    attended = attend(query, key_value, frame_mask, tail_pairs, tail_mask)
    branch = jnp.einsum("fpc,cd->fpd", attended, output_weight, preferred_element_type=jnp.float32)
    mixed = (
        (flat.astype(jnp.float32) + branch)
        .astype(jnp.bfloat16)
        .reshape(frames, rows, width, channels)
    )
    border = extended_2(mixed, (("tm", 1),), 1)
    hidden = convolve(border, first_kernel, first_bias).astype(jnp.bfloat16)
    hidden_border = extended_2(hidden, (("tm", 1),), 1)
    outcome = convolve(hidden_border, second_kernel, second_bias)
    return outcome.astype(jnp.bfloat16).reshape(frames, rows, width * second_kernel.shape[2])


def solution(mesh):
    placed = (P("row", "tm", None, None), P("row"), P(), P(), P(), P(), P(), P(), P())
    return jax.shard_map(
        body, mesh=mesh, in_specs=placed, out_specs=P("row", "tm", None), check_vma=False
    )
```

profile of v0, /device:TPU:4, one launch (start us, length us, event | category | flops | bytes accessed | tf_op | source)
XLA Modules:
  0.0 124.8 jit_solution(3844653455090829094)
XLA Ops:
  0.0 1.8 %convert_reduce_fusion = f32[32,2,37]{0,2,1:T(8,128)S(1)} fusion(bf16[32,2,37,256]{3,1,2,0:T(2,128)(2,1)} %param.9), kind=kLoop, calls=%fused_computation.31 | loop fusion | flops 1210048 | bytes 1221888 | tf_op jit(solution)/shard_map/reduce_sum | solution.py:40
  1.8 2.0 %fusion.19 = f32[32,2,37]{0,2,1:T(8,128)S(1)} fusion(f32[32,2,37]{0,2,1:T(8,128)S(1)} %broadcast_multiply_fusion, bf16[32,2,37,256]{3,1,2,0:T(2,128)(2,1)} %param.9), kind=kLoop, calls=%fused_computation.33 | loop fusion | flops 2422464 | bytes 1231360 | tf_op jit(solution)/shard_map/reduce_sum | solution.py:42
  3.9 0.9 fusion.22
  4.8 1.8 %slice.206 = bf16[31,74,256]{2,0,1:T(8,128)(2,1)} slice(bf16[32,74,256]{2,0,1:T(8,128)(2,1)S(1)} %fusion.22), slice={[1:32], [0:74], [0:256]} | slice | bytes 2349056 | tf_op jit(solution)/shard_map/slice | solution.py:122
  6.6 1.9 %collective-permute-start = (bf16[31,74,256]{2,0,1:T(8,128)(2,1)}, bf16[31,74,256]{2,0,1:T(8,128)(2,1)}, u32[]{:S(2)}, u32[]{:S(2)}) collective-permute-start(bf16[31,74,256]{2,0,1:T(8,128)(2,1)} %slice.206), channel_id=1, source_target_pairs={{0,1},{1,2},{2,3},{3,4},{4,5},{5,6},{6,7},{8,9},{9,10},{10,11},{11... | collective-permute-start | bytes 3523592 | tf_op jit(solution)/shard_map/ppermute | solution.py:18
  8.5 0.1 slice.165
  8.6 3.5 %collective-permute-start.1 = (s32[31]{0:T(128)S(1)}, s32[31]{0:T(128)S(1)}, u32[]{:S(2)}, u32[]{:S(2)}) collective-permute-start(s32[31]{0:T(128)S(1)} %slice.165), channel_id=1, source_target_pairs={{0,1},{1,2},{2,3},{3,4},{4,5},{5,6},{6,7},{8,9},{9,10},{10,11},{11... | collective-permute-start | bytes 380 | tf_op jit(solution)/shard_map/ppermute | solution.py:18
  12.1 2.2 %convolution_convert_fusion = bf16[32,74,768]{2,1,0:T(8,128)(2,1)S(1)} fusion(bf16[32,74,256]{2,0,1:T(8,128)(2,1)S(1)} %fusion.22, bf16[256,768]{1,0:T(8,128)(2,1)S(1)} %copy-done.5), kind=kOutput, calls=%fused_computation.27 | convolution fusion | flops 932954112 | bytes 5242880 | tf_op jit(solution)/shard_map/fpc,cd->fpd/dot_general | solution.py:116
  14.3 0.3 slice.207
  14.7 1.2 slice.209
  15.9 0.6 copy-done.2
  16.4 1.4 %copy.111 = bf16[32,2,37,256]{3,0,2,1:T(8,128)(2,1)} copy(bf16[32,2,37,256]{3,1,2,0:T(2,128)(2,1)S(1)} %copy-done.2) | data formatting | bytes 2424832 | tf_op args[0]
  17.8 3.8 %copy.119 = bf16[32,74,256]{1,2,0:T(8,128)(2,1)} copy(bf16[32,74,256]{2,1,0:T(8,128)(2,1)} %slice.209) | data formatting | bytes 2424832 | tf_op jit(solution)/shard_map/slice | solution.py:119
  21.6 0.1 pad_add_fusion.1
  21.6 1.8 %pad_slice_fusion = bf16[32,74,512]{2,1,0:T(8,128)(2,1)} fusion(bf16[32,74,512]{2,1,0:T(8,128)(2,1)S(1)} %slice.207), kind=kLoop, calls=%fused_computation.23 | loop fusion | bytes 4849664 | tf_op jit(solution)/shard_map/while/body/eval_jaxpr/dynamic_slice | solution.py:80
  23.4 7.2 %copy.121 = bf16[32,74,8,32]{3,0,2,1:T(8,128)(2,1)} copy(bf16[32,74,8,32]{1,3,2,0:T(8,128)(2,1)} %bitcast.170) | data formatting | bytes 2424832 | tf_op jit(solution)/shard_map/while/body/eval_jaxpr/squeeze | solution.py:85
  30.7 0.1 dynamic_slice.24
  30.7 0.1 pad_add_fusion
  30.8 0.1 add_compare_fusion
  30.9 0.1 fusion.110
  31.0 2.5 %convolution_convert_fusion.1 = bf16[31,74,512]{2,1,0:T(8,128)(2,1)S(1)} fusion(bf16[31,74,256]{2,0,1:T(8,128)(2,1)} %collective-permute-done, bf16[256,768]{1,0:T(8,128)(2,1)S(1)} %copy-done.5), kind=kOutput, calls=%fused_computation.38 | convolution fusion | flops 602532864 | bytes 3785728 | tf_op jit(solution)/shard_map/fpc,cd->fpd/dot_general | solution.py:124
  33.5 7.5 %fusion.4 = bf16[64,74,512]{2,1,0:T(8,128)(2,1)S(1)} fusion(bf16[32,74,512]{2,1,0:T(8,128)(2,1)S(1)} %slice.207, bf16[31,74,512]{2,1,0:T(8,128)(2,1)S(1)} %convolution_convert_fusion.1, bf16[32,74,512]{2,1,0:T(8,128)(2,1)S(1)} %copy-done.3), kind=kLoop, calls=%fused_computation.10 | loop fusion | flops 19398656 | bytes 12048384 | tf_op jit(solution)/shard_map/while/body/eval_jaxpr/concatenate | solution.py:80
  41.0 1.9 %fusion.137 = (bf16[64,74,256]{2,1,0:T(8,128)(2,1)}, bf16[64,74,256]{2,1,0:T(8,128)(2,1)S(1)}) fusion(bf16[64,74,512]{2,1,0:T(8,128)(2,1)S(1)} %fusion.4), kind=kLoop, calls=%fused_computation.161 | loop fusion | bytes 9699328 | tf_op jit(solution)/shard_map/while/body/eval_jaxpr/slice | solution.py:82
  43.0 6.5 %copy.159 = bf16[64,74,256]{0,2,1:T(8,128)(2,1)} copy(bf16[64,74,256]{2,1,0:T(8,128)(2,1)} %get-tuple-element.17) | data formatting | bytes 4849664 | tf_op jit(solution)/shard_map/while/body/eval_jaxpr/reshape | solution.py:82
  49.5 4.7 %copy.158 = bf16[64,74,256]{0,2,1:T(8,128)(2,1)} copy(bf16[64,74,256]{2,1,0:T(8,128)(2,1)S(1)} %get-tuple-element.18) | data formatting | bytes 4849664 | tf_op jit(solution)/shard_map/while/body/eval_jaxpr/reshape | solution.py:83
  54.1 10.5 %fusion.140 = (f32[74,8,32]{2,1,0:T(8,128)S(1)}, f32[74,8,32,64]{3,2,1,0:T(8,128)}) fusion(pred[32,64]{1,0:T(8,128)(4,1)S(1)} %fusion.110, bf16[32,74,8,32]{3,0,2,1:T(8,128)(2,1)} %copy.121, bf16[64,74,8,32]{0,3,2,1:T(8,128)(2,1)} %bitcast.171), kind=kOutput, calls=%fused_computation.164 | convolution fusion | flops 82444352 | bytes 8564736 | tf_op jit(solution)/shard_map/while/body/eval_jaxpr/sub | solution.py:90
  64.6 6.8 %fusion.14 = bf16[74,8,32,32]{3,2,1,0:T(8,128)(2,1)S(1)} fusion(bf16[64,74,8,32]{0,3,2,1:T(8,128)(2,1)} %bitcast.172, f32[74,8,32,64]{3,2,1,0:T(8,128)} %get-tuple-element.33, f32[74,8,32]{2,1,0:T(8,128)S(1)} %get-tuple-element.32), kind=kOutput, calls=%fused_computation.22 | convolution fusion | flops 80625664 | bytes 8562688 | tf_op jit(solution)/shard_map/while/body/eval_jaxpr/phij,jphd->iphd/dot_general | solution.py:92
  71.5 1.4 %fusion.23 = bf16[32,74,256]{2,0,1:T(8,128)(2,1)S(1)} fusion(bf16[32,2,37,256]{3,0,2,1:T(8,128)(2,1)S(1)} %copy-done.4, bf16[32,74,256]{0,2,1:T(8,128)(2,1)S(1)} %bitcast.173, bf16[256,256]{1,0:T(8,128)(2,1)S(1)} %copy-done), kind=kOutput, calls=%fused_computation.37 | convolution fusion | flops 312197120 | bytes 3768320 | tf_op jit(solution)/shard_map/fpc,cd->fpd/dot_general | solution.py:128
  72.9 0.1 fusion.138
  73.0 3.7 %collective-permute-start.2 = (bf16[32,1,37,256]{3,0,2,1:T(8,128)(2,1)S(1)}, bf16[32,1,37,256]{3,0,2,1:T(8,128)(2,1)S(1)}, u32[]{:S(2)}, u32[]{:S(2)}) collective-permute-start(bf16[32,1,37,256]{3,0,2,1:T(8,128)(2,1)S(1)} %get-tuple-element.19), channel_id=1, source_target_pairs={{0,8},{8,16},{16,24},{1,9},{9,17},{17,25},{2,10},{10,18},{18,26},{... | collective-permute-start | bytes 1818632 | tf_op jit(solution)/shard_map/ppermute | solution.py:29
  76.7 1.3 %collective-permute-start.3 = (bf16[32,1,37,256]{3,0,2,1:T(8,128)(2,1)S(1)}, bf16[32,1,37,256]{3,0,2,1:T(8,128)(2,1)S(1)}, u32[]{:S(2)}, u32[]{:S(2)}) collective-permute-start(bf16[32,1,37,256]{3,0,2,1:T(8,128)(2,1)S(1)} %get-tuple-element.20), channel_id=1, source_target_pairs={{8,0},{16,8},{24,16},{9,1},{17,9},{25,17},{10,2},{18,10},{26,18},{... | collective-permute-start | bytes 1818632 | tf_op jit(solution)/shard_map/ppermute | solution.py:31
  78.0 0.7 copy.127
  78.7 1.6 %fusion.94 = f32[32,2,37,128]{3,2,1,0:T(8,128)S(1)} fusion(bf16[9,256,128]{2,1,0:T(8,128)(2,1)S(1)} %copy-done.6, bf16[32,2,37,256]{3,0,2,1:T(8,128)(2,1)S(1)} %bitcast.169), kind=kOutput, calls=%fused_computation.109 | convolution fusion | flops 155189248 | bytes 2490368 | tf_op jit(solution)/shard_map/frwc,cd->frwd/dot_general | solution.py:54
  80.2 9.5 %collective-permute-done.2 = bf16[32,1,37,256]{3,0,2,1:T(8,128)(2,1)S(1)} collective-permute-done((bf16[32,1,37,256]{3,0,2,1:T(8,128)(2,1)S(1)}, bf16[32,1,37,256]{3,0,2,1:T(8,128)(2,1)S(1)}, u32[]{:S(2)}, u32[]{:S(2)}) %collective-permute-start.2) | collective-permute-done | bytes 606240 | tf_op jit(solution)/shard_map/ppermute | solution.py:29
  89.7 0.3 copy.126
  90.1 0.5 fusion.24
  90.6 3.3 %collective-permute-done.3 = bf16[32,1,37,256]{3,0,2,1:T(8,128)(2,1)S(1)} collective-permute-done((bf16[32,1,37,256]{3,0,2,1:T(8,128)(2,1)S(1)}, bf16[32,1,37,256]{3,0,2,1:T(8,128)(2,1)S(1)}, u32[]{:S(2)}, u32[]{:S(2)}) %collective-permute-start.3) | collective-permute-done | bytes 606240 | tf_op jit(solution)/shard_map/ppermute | solution.py:31
  93.9 0.3 copy.128
  94.2 1.5 %fusion.16 = bf16[32,4,39,256]{3,2,1,0:T(8,128)(2,1)S(1)} fusion(bf16[32,1,37,256]{3,2,1,0:T(8,128)(2,1)S(1)} %copy.128, bf16[32,2,37,256]{3,2,1,0:T(8,128)(2,1)S(1)} %copy.127, bf16[32,1,37,256]{3,2,1,0:T(8,128)(2,1)S(1)} %copy.126), kind=kLoop, calls=%fused_computation.25 | loop fusion | flops 15335424 | bytes 4980736 | tf_op jit(solution)/shard_map/concatenate | solution.py:27
  95.7 0.5 fusion.51
  96.2 0.5 fusion.53
  96.7 0.5 fusion.28
  97.3 0.5 fusion.46
  97.8 0.5 fusion.48
  98.4 0.6 fusion.66
  99.0 0.1 copy-done.9
  99.0 0.8 fusion.43
  99.8 0.1 fusion.139
  99.9 3.5 %collective-permute-start.4 = (bf16[32,1,37,128]{3,2,1,0:T(8,128)(2,1)S(1)}, bf16[32,1,37,128]{3,2,1,0:T(8,128)(2,1)S(1)}, u32[]{:S(2)}, u32[]{:S(2)}) collective-permute-start(bf16[32,1,37,128]{3,2,1,0:T(8,128)(2,1)S(1)} %get-tuple-element.28), channel_id=1, source_target_pairs={{0,8},{8,16},{16,24},{1,9},{9,17},{17,25},{2,10},{10,18},{18,26},{... | collective-permute-start | bytes 909320 | tf_op jit(solution)/shard_map/ppermute | solution.py:29
  103.4 1.6 %collective-permute-start.5 = (bf16[32,1,37,128]{3,2,1,0:T(8,128)(2,1)S(1)}, bf16[32,1,37,128]{3,2,1,0:T(8,128)(2,1)S(1)}, u32[]{:S(2)}, u32[]{:S(2)}) collective-permute-start(bf16[32,1,37,128]{3,2,1,0:T(8,128)(2,1)S(1)} %get-tuple-element.30), channel_id=1, source_target_pairs={{8,0},{16,8},{24,16},{9,1},{17,9},{25,17},{10,2},{18,10},{26,18},{... | collective-permute-start | bytes 909320 | tf_op jit(solution)/shard_map/ppermute | solution.py:31
  105.0 4.4 %collective-permute-done.4 = bf16[32,1,37,128]{3,2,1,0:T(8,128)(2,1)S(1)} collective-permute-done((bf16[32,1,37,128]{3,2,1,0:T(8,128)(2,1)S(1)}, bf16[32,1,37,128]{3,2,1,0:T(8,128)(2,1)S(1)}, u32[]{:S(2)}, u32[]{:S(2)}) %collective-permute-start.4) | collective-permute-done | bytes 303136 | tf_op jit(solution)/shard_map/ppermute | solution.py:29
  109.3 4.1 %collective-permute-done.5 = bf16[32,1,37,128]{3,2,1,0:T(8,128)(2,1)S(1)} collective-permute-done((bf16[32,1,37,128]{3,2,1,0:T(8,128)(2,1)S(1)}, bf16[32,1,37,128]{3,2,1,0:T(8,128)(2,1)S(1)}, u32[]{:S(2)}, u32[]{:S(2)}) %collective-permute-start.5) | collective-permute-done | bytes 303136 | tf_op jit(solution)/shard_map/ppermute | solution.py:31
  113.5 0.7 fusion.45
  114.2 1.0 fusion.79
  115.2 0.9 fusion.72
  116.1 1.0 convolution_add_fusion.7
  117.1 1.0 convolution_add_fusion.6
  118.1 1.0 convolution_add_fusion.5
  119.1 1.0 convolution_add_fusion.4
  120.1 1.0 convolution_add_fusion.3
  121.1 1.0 convolution_add_fusion.2
  122.1 1.0 fusion.70
  123.1 0.5 copy.160
  123.6 1.2 reshape.185
  (29 shorter events, 0.1 us)
Async XLA Ops:
  0.0 71.5 %copy-start = (bf16[256,256]{1,0:T(8,128)(2,1)S(1)}, bf16[256,256]{1,0:T(8,128)(2,1)}, u32[]{:S(2)}) copy-start(bf16[256,256]{1,0:T(8,128)(2,1)} %param.13) | copy-start | bytes 393220
  0.0 3.9 %copy-start.1 = (bf16[32,2,37,256]{3,1,2,0:T(2,128)(2,1)S(1)}, bf16[32,2,37,256]{3,1,2,0:T(2,128)(2,1)}, u32[]{:S(2)}) copy-start(bf16[32,2,37,256]{3,1,2,0:T(2,128)(2,1)} %param.9) | copy-start | bytes 3637252
  0.0 3.9 %copy-start.8 = (f32[256]{0:T(256)S(1)}, f32[256]{0:T(256)}, u32[]{:S(2)}) copy-start(f32[256]{0:T(256)} %param.11) | copy-start | bytes 3076
  3.9 4.6 %copy-start.11 = (s32[32]{0:T(128)S(1)}, s32[32]{0:T(128)}, u32[]{:S(2)}) copy-start(s32[32]{0:T(128)} %param.10) | copy-start | bytes 388
  3.9 8.2 %copy-start.5 = (bf16[256,768]{1,0:T(8,128)(2,1)S(1)}, bf16[256,768]{1,0:T(8,128)(2,1)}, u32[]{:S(2)}) copy-start(bf16[256,768]{1,0:T(8,128)(2,1)} %param.12) | copy-start | bytes 1179652
  6.6 24.4 %collective-permute-start = (bf16[31,74,256]{2,0,1:T(8,128)(2,1)}, bf16[31,74,256]{2,0,1:T(8,128)(2,1)}, u32[]{:S(2)}, u32[]{:S(2)}) collective-permute-start(bf16[31,74,256]{2,0,1:T(8,128)(2,1)} %slice.206), channel_id=1, source_target_pairs={{0,1},{1,2},{2,3},{3,4},{4,5},{5,6},{6,7},{8,9},{9,10},{10,11},{11... | collective-permute-start | bytes 3523592 | tf_op jit(solution)/shard_map/ppermute | solution.py:18
  8.6 22.1 %collective-permute-start.1 = (s32[31]{0:T(128)S(1)}, s32[31]{0:T(128)S(1)}, u32[]{:S(2)}, u32[]{:S(2)}) collective-permute-start(s32[31]{0:T(128)S(1)} %slice.165), channel_id=1, source_target_pairs={{0,1},{1,2},{2,3},{3,4},{4,5},{5,6},{6,7},{8,9},{9,10},{10,11},{11... | collective-permute-start | bytes 380 | tf_op jit(solution)/shard_map/ppermute | solution.py:18
  14.7 1.8 %copy-start.2 = (bf16[32,2,37,256]{3,1,2,0:T(2,128)(2,1)S(1)}, bf16[32,2,37,256]{3,1,2,0:T(2,128)(2,1)}, u32[]{:S(2)}) copy-start(bf16[32,2,37,256]{3,1,2,0:T(2,128)(2,1)} %param.9) | copy-start | bytes 3637252
  30.7 2.8 %copy-start.3 = (bf16[32,74,512]{2,1,0:T(8,128)(2,1)S(1)}, bf16[32,74,512]{2,1,0:T(8,128)(2,1)}, u32[]{:S(2)}) copy-start(bf16[32,74,512]{2,1,0:T(8,128)(2,1)} %pad_slice_fusion) | copy-start | bytes 7274500
  64.6 6.8 %copy-start.4 = (bf16[32,2,37,256]{3,0,2,1:T(8,128)(2,1)S(1)}, bf16[32,2,37,256]{3,0,2,1:T(8,128)(2,1)}, u32[]{:S(2)}) copy-start(bf16[32,2,37,256]{3,0,2,1:T(8,128)(2,1)} %copy.111) | copy-start | bytes 3637252
  72.9 5.8 %copy-start.6 = (bf16[9,256,128]{2,1,0:T(8,128)(2,1)S(1)}, bf16[9,256,128]{2,1,0:T(8,128)(2,1)}, u32[]{:S(2)}) copy-start(bf16[9,256,128]{2,1,0:T(8,128)(2,1)} %param.14) | copy-start | bytes 1769476
  73.0 16.7 %collective-permute-start.2 = (bf16[32,1,37,256]{3,0,2,1:T(8,128)(2,1)S(1)}, bf16[32,1,37,256]{3,0,2,1:T(8,128)(2,1)S(1)}, u32[]{:S(2)}, u32[]{:S(2)}) collective-permute-start(bf16[32,1,37,256]{3,0,2,1:T(8,128)(2,1)S(1)} %get-tuple-element.19), channel_id=1, source_target_pairs={{0,8},{8,16},{16,24},{1,9},{9,17},{17,25},{2,10},{10,18},{18,26},{... | collective-permute-start | bytes 1818632 | tf_op jit(solution)/shard_map/ppermute | solution.py:29
  76.7 17.2 %collective-permute-start.3 = (bf16[32,1,37,256]{3,0,2,1:T(8,128)(2,1)S(1)}, bf16[32,1,37,256]{3,0,2,1:T(8,128)(2,1)S(1)}, u32[]{:S(2)}, u32[]{:S(2)}) collective-permute-start(bf16[32,1,37,256]{3,0,2,1:T(8,128)(2,1)S(1)} %get-tuple-element.20), channel_id=1, source_target_pairs={{8,0},{16,8},{24,16},{9,1},{17,9},{25,17},{10,2},{18,10},{26,18},{... | collective-permute-start | bytes 1818632 | tf_op jit(solution)/shard_map/ppermute | solution.py:31
  98.4 0.7 copy-start.9
  99.8 14.3 %copy-start.7 = (bf16[9,128,32]{1,2,0:T(8,128)(2,1)S(1)}, bf16[9,128,32]{1,2,0:T(8,128)(2,1)}, u32[]{:S(2)}) copy-start(bf16[9,128,32]{1,2,0:T(8,128)(2,1)} %param.16) | copy-start | bytes 221188
  99.9 9.4 %collective-permute-start.4 = (bf16[32,1,37,128]{3,2,1,0:T(8,128)(2,1)S(1)}, bf16[32,1,37,128]{3,2,1,0:T(8,128)(2,1)S(1)}, u32[]{:S(2)}, u32[]{:S(2)}) collective-permute-start(bf16[32,1,37,128]{3,2,1,0:T(8,128)(2,1)S(1)} %get-tuple-element.28), channel_id=1, source_target_pairs={{0,8},{8,16},{16,24},{1,9},{9,17},{17,25},{2,10},{10,18},{18,26},{... | collective-permute-start | bytes 909320 | tf_op jit(solution)/shard_map/ppermute | solution.py:29
  103.4 10.1 %collective-permute-start.5 = (bf16[32,1,37,128]{3,2,1,0:T(8,128)(2,1)S(1)}, bf16[32,1,37,128]{3,2,1,0:T(8,128)(2,1)S(1)}, u32[]{:S(2)}, u32[]{:S(2)}) collective-permute-start(bf16[32,1,37,128]{3,2,1,0:T(8,128)(2,1)S(1)} %get-tuple-element.30), channel_id=1, source_target_pairs={{8,0},{16,8},{24,16},{9,1},{17,9},{25,17},{10,2},{18,10},{26,18},{... | collective-permute-start | bytes 909320 | tf_op jit(solution)/shard_map/ppermute | solution.py:31
  120.1 2.0 %copy-start.10 = (f32[32]{0:T(128)S(1)}, f32[32]{0:T(128)}, u32[]{:S(2)}) copy-start(f32[32]{0:T(128)} %param.17) | copy-start | bytes 388
where the time goes:
time: 127 us; the launch traced here: 125 us
  matrix products  38.4 us (30%)
  local copies, waits for them, and re-layouts  34.6 us (27%)
  waiting for transfers between devices  21.3 us (17%)
  starting transfers between devices  15.4 us (12%)
  other arithmetic  14.8 us (12%)
    dot_general x18, matrix products, convolve(): jnp.einsum('frwc,cd->frwd', window, kernel[3 * tap_row + tap_col], prefer...  14.9 us
    ppermute x2, waiting for transfers between devices, extended_2(): lax.ppermute(tail, axis, [(i, (i + 1) % count) for i in range(ends)])  13.9 us
    sub x1, matrix products, one_block(): powers = jnp.exp(scores - largest)  10.5 us
    concatenate x1, other arithmetic, one_block(): paired = jnp.concatenate([blocks[block_id], blocks[block_id + 1]], axis=0)  7.53 us
    ppermute x2, waiting for transfers between devices, extended_2(): lax.ppermute(head, axis, [((i + 1) % count, i) for i in range(ends)])  7.43 us
    squeeze x1, local copies, waits for them, and re-layouts, one_block(): query_blocks[block_id]  7.22 us
    ppermute x2, starting transfers between devices, extended_2(): lax.ppermute(tail, axis, [(i, (i + 1) % count) for i in range(ends)])  7.15 us
    dot_general x1, matrix products, one_block(): jnp.einsum('phij,jphd->iphd', weights, value_part, preferred_element_type...  6.82 us
  transfers between devices with their start and end apart: 6, of which 4 were waited for; matrix products, arithmetic and copies ran while one was open for 17% of the time, Pallas kernels for 0%

commit v1 on v0

v1 whole, which is shorter than its diff:
```python
import functools
import math

import jax
import jax.numpy as jnp
from jax import lax
from jax.experimental import pallas as pl
from jax.experimental.pallas import tpu as pltpu
from jax.sharding import PartitionSpec as P

HEADS = 8
WIN = 32
TAPS = 3
GROUP = 4
NEG = -1e30
epsilon = 1e-05
MESH = pl.DeviceIdType.MESH
F32 = jnp.float32
BF16 = jnp.bfloat16


def layer_norm(field, gain):
    widened = field.astype(F32)
    average = jnp.mean(widened, axis=-1, keepdims=True)
    centered = widened - average
    variance = jnp.mean(centered * centered, axis=-1, keepdims=True)
    return (centered * lax.rsqrt(variance + epsilon) * gain).astype(BF16)


def dot(a, b):
    return jnp.dot(a, b, preferred_element_type=F32)


def dot_t(a, b):
    return lax.dot_general(a, b, (((1,), (1,)), ((), ())), preferred_element_type=F32)


def dot_tt(a, b):
    return lax.dot_general(a, b, (((0,), (0,)), ((), ())), preferred_element_type=F32)


def kernel(
    width,
    bounds,
    n_row,
    n_tm,
    x_ref,
    mask_ref,
    gain_ref,
    win_ref,
    wout_ref,
    k1_ref,
    b1_ref,
    k2_ref,
    b2_ref,
    o_ref,
    halo,
    pmask,
    qkv,
    hkv,
    att,
    headmask,
    bias,
    grid_x,
    w1,
    w2,
    acc,
    p_up,
    p_down,
    r_up,
    r_down,
    hid,
    acc2,
    s_up,
    s_down,
    t_up,
    t_down,
    send_sem,
    recv_sem,
):
    frames = WIN
    channels = x_ref.shape[1]
    head_size = channels // HEADS
    half = HEADS // 2
    tokens = width * frames
    c1 = k1_ref.shape[2]
    c2 = k2_ref.shape[1]
    row = lax.axis_index("row")
    tm = lax.axis_index("tm")
    has_prev, has_next = row > 0, row < n_row - 1
    has_up, has_down = tm > 0, tm < n_tm - 1

    barrier = pltpu.get_barrier_semaphore()
    sides = (
        (has_prev, {"row": row - 1}),
        (has_next, {"row": row + 1}),
        (has_up, {"tm": tm - 1}),
        (has_down, {"tm": tm + 1}),
    )
    for present, where in sides:

        @pl.when(present)
        def _(where=where):
            pl.semaphore_signal(barrier, inc=1, device_id=where, device_id_type=MESH)

    pl.semaphore_wait(barrier, sum(present.astype(jnp.int32) for present, _ in sides))

    def copy(src, dst, slot, where):
        return pltpu.make_async_remote_copy(
            src_ref=src,
            dst_ref=dst,
            send_sem=send_sem.at[slot],
            recv_sem=recv_sem.at[slot],
            device_id=where,
            device_id_type=MESH,
        )

    nxt = {"row": row + 1}
    chunks = len(bounds) - 1
    halo_copies = [copy(mask_ref, pmask, chunks, nxt)]
    for c in range(chunks):
        part = pl.ds(bounds[c] * frames, (bounds[c + 1] - bounds[c]) * frames)
        halo_copies.append(copy(x_ref.at[part], halo.at[part], c, nxt))

    @pl.when(has_next)
    def _():
        for one in halo_copies:
            one.start()

    @pl.when(jnp.logical_not(has_prev))
    def _():
        halo[...] = jnp.zeros_like(halo)
        pmask[...] = jnp.zeros_like(pmask)

    up, down = {"tm": tm - 1}, {"tm": tm + 1}
    first_up = copy(p_up, r_down, chunks + 1, up)
    first_down = copy(p_down, r_up, chunks + 2, down)
    second_up = copy(s_up, t_down, chunks + 3, up)
    second_down = copy(s_down, t_up, chunks + 4, down)

    for tap in range(TAPS * TAPS):
        a, b = tap // TAPS, tap % TAPS
        w1[b * channels : (b + 1) * channels, a * c1 : (a + 1) * c1] = k1_ref[tap]
    w2[...] = jnp.zeros_like(w2)
    for a in range(TAPS):
        for o in range(GROUP):
            for b in range(TAPS):
                r0 = (a * GROUP + o) * c2
                w2[r0 : r0 + c2, (o + b) * c1 : (o + b + 1) * c1] = k2_ref[a * TAPS + b]
    for r in range(2):
        grid_x[r, 0:frames] = jnp.zeros((frames, channels), BF16)
        grid_x[r, tokens + frames : tokens + 2 * frames] = jnp.zeros((frames, channels), BF16)
        hid[r] = jnp.zeros_like(hid[r])

    lane = lax.broadcasted_iota(jnp.int32, (HEADS * frames, channels), 1)
    sub = lax.broadcasted_iota(jnp.int32, (HEADS * frames, channels), 0)
    headmask[...] = (lane // head_size == sub // frames).astype(F32).astype(BF16)

    gain = gain_ref[...]
    total = 2 * tokens
    block = total // 4

    def project(i, carry):
        at = pl.multiple_of(i * block, 16)
        normed = layer_norm(x_ref[pl.ds(at, block)], gain)
        qkv[pl.ds(at, block)] = dot(normed, win_ref[...]).astype(BF16)
        return carry

    lax.fori_loop(0, 4, project, 0)

    scale = 1.0 / math.sqrt(head_size)
    slot_s = lax.broadcasted_iota(jnp.int32, (frames, HEADS * frames), 0)
    slot_t = lax.broadcasted_iota(jnp.int32, (frames, HEADS * frames), 1) % frames
    own = slot_s <= slot_t

    @pl.when(has_prev)
    def _():
        halo_copies[0].wait_recv()

    m_own = jnp.concatenate([mask_ref[...]] * (HEADS * frames // 128), axis=1)
    m_prev = jnp.concatenate([pmask[...]] * (HEADS * frames // 128), axis=1)
    seen = jnp.where(own, jnp.where(slot_s == slot_t, 1.0, m_own), m_prev)
    bias[...] = jnp.where(seen == 1.0, 0.0, NEG)

    lane_head = lax.broadcasted_iota(jnp.int32, (frames, channels // 2), 1) // head_size

    def place(p):
        rows = pl.ds(pl.multiple_of(p * frames, frames), frames)
        q = qkv[rows, 0:channels]
        k = jnp.concatenate([hkv[rows, 0:channels], qkv[rows, channels : 2 * channels]], axis=0)
        v = jnp.concatenate(
            [hkv[rows, channels : 2 * channels], qkv[rows, 2 * channels : 3 * channels]], axis=0
        )
        spread = jnp.concatenate([q] * HEADS, axis=0) * headmask[...]
        s = dot_t(k, spread)
        s = jnp.where(own, s[frames:], s[:frames]) + bias[...]
        peak = jnp.max(s, axis=0, keepdims=True)
        powers = jnp.exp((s - peak) * scale)
        w = powers * (1.0 / jnp.sum(powers, axis=0, keepdims=True))
        w = jnp.concatenate([jnp.where(own, 0.0, w), jnp.where(own, w, 0.0)], axis=0).astype(BF16)
        outs = []
        for g in range(2):
            cols = slice(g * channels // 2, (g + 1) * channels // 2)
            r = dot_tt(w[:, g * half * frames : (g + 1) * half * frames], v[:, cols])
            total_g = r[0:frames]
            for h in range(1, half):
                total_g = jnp.where(lane_head == h, r[h * frames : (h + 1) * frames], total_g)
            outs.append(total_g)
        att[rows] = jnp.concatenate(outs, axis=1).astype(BF16)

    def pair(i, carry):
        place(2 * i)
        place(2 * i + 1)
        return carry

    tile = tokens // 2

    def finish(r):
        for i in range(2):
            rows = slice(r * tokens + i * tile, r * tokens + (i + 1) * tile)
            mixed = x_ref[rows].astype(F32) + dot(att[rows], wout_ref[...])
            grid_x[r, frames + i * tile : frames + (i + 1) * tile] = mixed.astype(BF16)
        for i in range(2):
            window = jnp.concatenate(
                [grid_x[r, b * frames + i * tile : b * frames + (i + 1) * tile] for b in range(TAPS)],
                axis=1,
            )
            full = dot(window, w1[...])
            rows = slice(i * tile, (i + 1) * tile)
            below, here, above = full[:, 0:c1], full[:, c1 : 2 * c1], full[:, 2 * c1 : 3 * c1]
            if r == 0:
                p_up[rows] = above.astype(BF16)
                acc[0, rows] = here
                acc[1, rows] = below
            else:
                p_down[rows] = below.astype(BF16)
                acc[1, rows] = acc[1, rows] + here
                acc[0, rows] = acc[0, rows] + above

    for c in range(chunks):

        @pl.when(has_prev)
        def _(c=c):
            halo_copies[c + 1].wait_recv()

        part = slice(bounds[c] * frames, bounds[c + 1] * frames)
        normed = layer_norm(halo[part], gain)
        hkv[part] = dot(normed, win_ref[:, channels : 3 * channels]).astype(BF16)
        lax.fori_loop(bounds[c] // 2, bounds[c + 1] // 2, pair, 0)
        if bounds[c] < width <= bounds[c + 1]:
            finish(0)

            @pl.when(has_up)
            def _():
                first_up.start()

    finish(1)

    @pl.when(has_down)
    def _():
        first_down.start()

    @pl.when(jnp.logical_not(has_up))
    def _():
        r_up[...] = jnp.zeros_like(r_up)
        t_up[...] = jnp.zeros_like(t_up)

    @pl.when(jnp.logical_not(has_down))
    def _():
        r_down[...] = jnp.zeros_like(r_down)
        t_down[...] = jnp.zeros_like(t_down)

    b2 = jnp.concatenate([b2_ref[...]] * GROUP, axis=1)
    groups = (width + GROUP - 1) // GROUP
    span = (GROUP + TAPS - 1) * c1

    def hidden_row(r, received):
        for col in range(width):
            rows = slice(col * frames, (col + 1) * frames)
            h = jnp.maximum(acc[r, rows] + received[rows].astype(F32) + b1_ref[...], 0.0)
            hid[r, :, (col + 1) * c1 : (col + 2) * c1] = h.astype(BF16)
        window = jnp.concatenate(
            [hid[r, :, g * GROUP * c1 : g * GROUP * c1 + span] for g in range(groups)], axis=0
        )
        full = dot_t(window, w2[...])
        n = GROUP * c2
        return full[:, 0:n], full[:, n : 2 * n], full[:, 2 * n : 3 * n]

    @pl.when(has_down)
    def _():
        first_up.wait_recv()

    below, here, above = hidden_row(1, r_down)
    s_down[...] = below.astype(BF16)
    acc2[1] = here
    acc2[0] = above

    @pl.when(has_down)
    def _():
        second_down.start()

    @pl.when(has_up)
    def _():
        first_down.wait_recv()

    below, here, above = hidden_row(0, r_up)
    s_up[...] = above.astype(BF16)
    acc2[0] = acc2[0] + here
    acc2[1] = acc2[1] + below

    @pl.when(has_up)
    def _():
        second_up.start()

    def final_row(r, received):
        out = jnp.maximum(acc2[r] + received[...].astype(F32) + b2, 0.0).astype(BF16)
        for g in range(groups):
            cols = min(GROUP, width - g * GROUP) * c2
            at = g * GROUP * c2
            o_ref[r, :, at : at + cols] = out[g * frames : (g + 1) * frames, 0:cols]

    @pl.when(has_up)
    def _():
        second_down.wait_recv()

    final_row(0, t_up)

    @pl.when(has_down)
    def _():
        second_up.wait_recv()

    final_row(1, t_down)

    @pl.when(has_next)
    def _():
        for one in halo_copies:
            one.wait_send()

    @pl.when(has_up)
    def _():
        first_up.wait_send()
        second_up.wait_send()

    @pl.when(has_down)
    def _():
        first_down.wait_send()
        second_down.wait_send()


def body(
    n_row,
    n_tm,
    features,
    frame_mask,
    norm_gain,
    input_weight,
    output_weight,
    first_kernel,
    first_bias,
    second_kernel,
    second_bias,
):
    frames, rows, width, channels = features.shape
    assert frames == WIN and rows == 2
    places = rows * width
    tokens = width * frames
    c1 = first_kernel.shape[2]
    c2 = second_kernel.shape[2]
    groups = (width + GROUP - 1) // GROUP
    x = features.transpose(1, 2, 0, 3).reshape(places * frames, channels)
    mask = jnp.broadcast_to(frame_mask.astype(F32)[:, None], (frames, 128))
    step = 2 * (places // 8)
    bounds = tuple(places - i * step for i in (4, 3, 2, 1, 0))
    bounds = (0,) + bounds[1:]
    slots = len(bounds) + 4
    vmem = pltpu.VMEM
    out = pl.pallas_call(
        functools.partial(kernel, width, bounds, n_row, n_tm),
        out_shape=jax.ShapeDtypeStruct((rows, frames, width * c2), BF16),
        in_specs=[pl.BlockSpec(memory_space=pltpu.VMEM)] * 9,
        out_specs=pl.BlockSpec(memory_space=pltpu.VMEM),
        scratch_shapes=[
            vmem((places * frames, channels), BF16),
            vmem((frames, 128), F32),
            vmem((places * frames, 3 * channels), BF16),
            vmem((places * frames, 2 * channels), BF16),
            vmem((places * frames, channels), BF16),
            vmem((HEADS * frames, channels), BF16),
            vmem((frames, HEADS * frames), F32),
            vmem((rows, tokens + 2 * frames, channels), BF16),
            vmem((TAPS * channels, TAPS * c1), BF16),
            vmem((TAPS * GROUP * c2, (GROUP + TAPS - 1) * c1), BF16),
            vmem((rows, tokens, c1), F32),
            vmem((tokens, c1), BF16),
            vmem((tokens, c1), BF16),
            vmem((tokens, c1), BF16),
            vmem((tokens, c1), BF16),
            vmem((rows, frames, (groups * GROUP + TAPS - 1) * c1), BF16),
            vmem((rows, groups * frames, GROUP * c2), F32),
            vmem((groups * frames, GROUP * c2), BF16),
            vmem((groups * frames, GROUP * c2), BF16),
            vmem((groups * frames, GROUP * c2), BF16),
            vmem((groups * frames, GROUP * c2), BF16),
            pltpu.SemaphoreType.DMA((slots,)),
            pltpu.SemaphoreType.DMA((slots,)),
        ],
        compiler_params=pltpu.CompilerParams(
            collective_id=0, has_side_effects=True, vmem_limit_bytes=60 * 1024 * 1024
        ),
    )(
        x,
        mask,
        norm_gain[None],
        input_weight,
        output_weight,
        first_kernel,
        first_bias[None],
        second_kernel.transpose(0, 2, 1),
        second_bias[None],
    )
    return out.transpose(1, 0, 2)


def solution(mesh):
    placed = (P("row", "tm", None, None), P("row"), P(), P(), P(), P(), P(), P(), P())
    return jax.shard_map(
        functools.partial(body, mesh.shape["row"], mesh.shape["tm"]),
        mesh=mesh,
        in_specs=placed,
        out_specs=P("row", "tm", None),
        check_vma=False,
    )
```

time: 127 us -> 59.5 us (0.47)
  the two profiles are of different devices: /device:TPU:4 before, /device:TPU:0 now
where the time goes in v1:
time: 59.5 us; the launch traced here: 59.3 us
  Pallas kernels  53.6 us (90%)
  local copies, waits for them, and re-layouts  4.96 us (8%)
  other arithmetic  0.66 us (1%)
    pallas_call x1, Pallas kernels, body(): pl.pallas_call(functools.partial(kernel, width, bounds, n_row, n_tm), out...  53.6 us
    transpose x1, local copies, waits for them, and re-layouts, body(): x = features.transpose(1, 2, 0, 3).reshape(places * frames, channels)  2.53 us
    transpose x1, local copies, waits for them, and re-layouts, body(): return out.transpose(1, 0, 2)  1.75 us

profile of v1, /device:TPU:0, one launch (start us, length us, event | category | flops | bytes accessed | tf_op | source)
XLA Modules:
  0.0 59.3 jit_solution(7631806510634703219)
XLA Ops:
  0.0 0.7 %convert_element_type.3 = f32[32]{0:T(128)S(1)} convert(s32[32]{0:T(128)} %param.10) | non-fusion elementwise | flops 32 | bytes 256 | tf_op jit(solution)/shard_map/convert_element_type | solution.py:371
  0.7 0.7 %broadcast_in_dim.15.mask_ref = f32[32,128]{1,0:T(8,128)} broadcast(f32[32]{0:T(128)S(1)} %convert_element_type.3), dimensions={0} | broadcast | bytes 16512 | tf_op jit(solution)/shard_map/broadcast_in_dim | solution.py:371
  1.3 2.5 %copy.10 = bf16[2,37,32,256]{3,2,1,0:T(8,128)(2,1)} copy(bf16[2,37,32,256]{3,0,1,2:T(2,128)(2,1)} %bitcast.8) | data formatting | bytes 2424832 | tf_op jit(solution)/shard_map/transpose | solution.py:370
  3.9 53.6 %shard_map.91 = bf16[2,32,1184]{2,1,0:T(8,128)(2,1)} custom-call(bf16[2368,256]{1,0:T(8,128)(2,1)} %bitcast.7, f32[32,128]{1,0:T(8,128)} %broadcast_in_dim.15.mask_ref, f32[1,256]{1,0:T(1,128)} %bitcast.11, bf16[256,768]{1,0:T(8,128)(2,1)} %win_ref.1, bf16[256,256]{1,0:T(8,128)(2,1)} %wout_ref.1, bf16[9,256,128]{2,1,0:T(8,128)(2,1)} %k1_ref.1, ...), custom_call_target="tpu_custom_call" | custom-call | tf_op jit(solution)/shard_map/pallas_call | solution.py:377
  57.5 1.8 %copy.11 = bf16[32,2,1184]{2,1,0:T(2,128)(2,1)} copy(bf16[32,2,1184]{2,0,1:T(8,128)(2,1)} %bitcast.9) | data formatting | bytes 303104 | tf_op jit(solution)/shard_map/transpose | solution.py:421

commit v2 on v1

v2 whole, which is shorter than its diff:
```python
import functools
import math

import jax
import jax.numpy as jnp
from jax import lax
from jax.experimental import pallas as pl
from jax.experimental.pallas import tpu as pltpu
from jax.sharding import PartitionSpec as P

HEADS = 8
WIN = 32
TAPS = 3
GROUP = 4
UNROLL = 4
CHUNKS = 4
NEG = -1e30
epsilon = 1e-05
MESH = pl.DeviceIdType.MESH
F32 = jnp.float32
BF16 = jnp.bfloat16


def layer_norm(field, gain):
    widened = field.astype(F32)
    average = jnp.mean(widened, axis=-1, keepdims=True)
    centered = widened - average
    variance = jnp.mean(centered * centered, axis=-1, keepdims=True)
    return (centered * lax.rsqrt(variance + epsilon) * gain).astype(BF16)


def dot(a, b):
    return jnp.dot(a, b, preferred_element_type=F32)


def dot_t(a, b):
    return lax.dot_general(a, b, (((1,), (1,)), ((), ())), preferred_element_type=F32)


def dot_tt(a, b):
    return lax.dot_general(a, b, (((0,), (0,)), ((), ())), preferred_element_type=F32)


def kernel(
    width,
    bounds,
    n_row,
    n_tm,
    x_ref,
    mask_ref,
    gain_ref,
    win_ref,
    wout_ref,
    k1_ref,
    b1_ref,
    k2_ref,
    b2_ref,
    o_ref,
    nrm,
    halo,
    pmask,
    qkv,
    hkv,
    att,
    headmask,
    bias,
    grid_x,
    w1,
    w2,
    acc,
    p_up,
    p_down,
    r_up,
    r_down,
    hid,
    acc2,
    s_up,
    s_down,
    t_up,
    t_down,
    send_sem,
    recv_sem,
):
    frames = WIN
    both = 2 * frames
    channels = x_ref.shape[1]
    head_size = channels // HEADS
    half = HEADS // 2
    c1 = k1_ref.shape[2]
    c2 = k2_ref.shape[1]
    row = lax.axis_index("row")
    tm = lax.axis_index("tm")
    has_prev, has_next = row > 0, row < n_row - 1
    has_up, has_down = tm > 0, tm < n_tm - 1
    chunks = len(bounds) - 1
    groups = (width + GROUP - 1) // GROUP
    edges = (0,) + tuple(b - 1 for b in bounds[1:-1]) + (width,)
    packs = (0,) + tuple((e - 1) // GROUP for e in edges[1:-1]) + (groups,)

    barrier = pltpu.get_barrier_semaphore()
    sides = (
        (has_prev, {"row": row - 1}),
        (has_next, {"row": row + 1}),
        (has_up, {"tm": tm - 1}),
        (has_down, {"tm": tm + 1}),
    )
    for present, where in sides:

        @pl.when(present)
        def _(where=where):
            pl.semaphore_signal(barrier, inc=1, device_id=where, device_id_type=MESH)

    pl.semaphore_wait(barrier, sum(present.astype(jnp.int32) for present, _ in sides))

    def copy(src, dst, slot, where):
        return pltpu.make_async_remote_copy(
            src_ref=src,
            dst_ref=dst,
            send_sem=send_sem.at[slot],
            recv_sem=recv_sem.at[slot],
            device_id=where,
            device_id_type=MESH,
        )

    nxt, up, down = {"row": row + 1}, {"tm": tm - 1}, {"tm": tm + 1}
    mask_copy = copy(mask_ref, pmask, 5 * chunks, nxt)
    halo_copies, first_up, first_down, second_up, second_down = [], [], [], [], []
    for c in range(chunks):
        part = pl.ds(bounds[c] * both, (bounds[c + 1] - bounds[c]) * both)
        halo_copies.append(copy(nrm.at[part], halo.at[part], c, nxt))
        part = pl.ds(edges[c] * frames, (edges[c + 1] - edges[c]) * frames)
        first_up.append(copy(p_up.at[part], r_down.at[part], chunks + c, up))
        first_down.append(copy(p_down.at[part], r_up.at[part], 2 * chunks + c, down))
        part = pl.ds(packs[c] * frames, (packs[c + 1] - packs[c]) * frames)
        second_up.append(copy(s_up.at[part], t_down.at[part], 3 * chunks + c, up))
        second_down.append(copy(s_down.at[part], t_up.at[part], 4 * chunks + c, down))

    def start(present, one):
        @pl.when(present)
        def _():
            one.start()

    def received(present, one):
        @pl.when(present)
        def _():
            one.wait_recv()

    start(has_next, mask_copy)

    @pl.when(jnp.logical_not(has_prev))
    def _():
        halo[...] = jnp.zeros_like(halo)
        pmask[...] = jnp.zeros_like(pmask)

    @pl.when(jnp.logical_not(has_up))
    def _():
        r_up[...] = jnp.zeros_like(r_up)
        t_up[...] = jnp.zeros_like(t_up)

    @pl.when(jnp.logical_not(has_down))
    def _():
        r_down[...] = jnp.zeros_like(r_down)
        t_down[...] = jnp.zeros_like(t_down)

    gain = gain_ref[...]
    for c in range(chunks):
        part = slice(bounds[c] * both, bounds[c + 1] * both)
        normed = layer_norm(x_ref[part], gain)
        nrm[part] = normed
        qkv[part] = dot(normed, win_ref[...]).astype(BF16)
        start(has_next, halo_copies[c])

    for tap in range(TAPS * TAPS):
        a, b = tap // TAPS, tap % TAPS
        w1[b * channels : (b + 1) * channels, a * c1 : (a + 1) * c1] = k1_ref[tap]
    w2[...] = jnp.zeros_like(w2)
    for a in range(TAPS):
        for o in range(GROUP):
            for b in range(TAPS):
                r0 = (a * GROUP + o) * c2
                w2[r0 : r0 + c2, (o + b) * c1 : (o + b + 1) * c1] = k2_ref[a * TAPS + b]
    end = width * both
    grid_x[0:both] = jnp.zeros((both, channels), BF16)
    grid_x[end + both : end + 2 * both] = jnp.zeros((both, channels), BF16)
    if qkv.shape[0] > end:
        qkv[end:] = jnp.zeros_like(qkv[end:])
        hkv[end:] = jnp.zeros_like(hkv[end:])
    for r in range(2):
        hid[r, :, 0:c1] = jnp.zeros((frames, c1), BF16)
        tail = hid.shape[2] - (width + 1) * c1
        hid[r, :, (width + 1) * c1 :] = jnp.zeros((frames, tail), BF16)

    lane = lax.broadcasted_iota(jnp.int32, (HEADS * frames, channels), 1)
    sub = lax.broadcasted_iota(jnp.int32, (HEADS * frames, channels), 0)
    headmask[...] = (lane // head_size == sub // frames).astype(F32).astype(BF16)

    scale = 1.0 / math.sqrt(head_size)
    slot_s = lax.broadcasted_iota(jnp.int32, (frames, HEADS * frames), 0)
    slot_t = lax.broadcasted_iota(jnp.int32, (frames, HEADS * frames), 1) % frames
    own = slot_s <= slot_t

    received(has_prev, mask_copy)
    eye_s = lax.broadcasted_iota(jnp.int32, (frames, frames), 0)
    eye_t = lax.broadcasted_iota(jnp.int32, (frames, frames), 1)

    def column(ref):
        spread = jnp.broadcast_to(ref[...].astype(F32), (frames, frames))
        picked = jnp.sum(jnp.where(eye_s == eye_t, spread, 0.0), axis=1, keepdims=True)
        return jnp.broadcast_to(picked, (frames, HEADS * frames))

    seen = jnp.where(own, jnp.where(slot_s == slot_t, 1.0, column(mask_ref)), column(pmask))
    bias[...] = jnp.where(seen == 1.0, 0.0, NEG)

    lane_head = lax.broadcasted_iota(jnp.int32, (frames, channels // 2), 1) // head_size

    def scores(p):
        rows = pl.ds(pl.multiple_of(p * frames, frames), frames)
        q = qkv[rows, 0:channels]
        k = jnp.concatenate([hkv[rows, 0:channels], qkv[rows, channels : 2 * channels]], axis=0)
        spread = jnp.concatenate([q] * HEADS, axis=0) * headmask[...]
        return dot_t(k, spread)

    def soften(s):
        s = jnp.where(own, s[frames:], s[:frames]) + bias[...]
        peak = jnp.max(s, axis=0, keepdims=True)
        powers = jnp.exp((s - peak) * scale)
        w = powers * (1.0 / jnp.sum(powers, axis=0, keepdims=True))
        return jnp.concatenate([jnp.where(own, 0.0, w), jnp.where(own, w, 0.0)], axis=0).astype(BF16)

    def gather(p, w):
        rows = pl.ds(pl.multiple_of(p * frames, frames), frames)
        v = jnp.concatenate(
            [hkv[rows, channels : 2 * channels], qkv[rows, 2 * channels : 3 * channels]], axis=0
        )
        outs = []
        for g in range(2):
            cols = slice(g * channels // 2, (g + 1) * channels // 2)
            r = dot_tt(w[:, g * half * frames : (g + 1) * half * frames], v[:, cols])
            total_g = r[0:frames]
            for h in range(1, half):
                total_g = jnp.where(lane_head == h, r[h * frames : (h + 1) * frames], total_g)
            outs.append(total_g)
        att[rows] = jnp.concatenate(outs, axis=1).astype(BF16)

    def step(i, carry):
        ids = [UNROLL * i + u for u in range(UNROLL)]
        raw = [scores(p) for p in ids]
        soft = [soften(s) for s in raw]
        for p, w in zip(ids, soft):
            gather(p, w)
        return carry

    b2 = jnp.concatenate([b2_ref[...]] * GROUP, axis=1)
    span = (GROUP + TAPS - 1) * c1

    def split(full, n):
        return full[:, 0:n], full[:, n : 2 * n], full[:, 2 * n : 3 * n]

    def convolve_first(c):
        lo, hi = edges[c], edges[c + 1]
        window = jnp.concatenate(
            [grid_x[(lo + b) * both : (hi + b) * both] for b in range(TAPS)], axis=1
        )
        below, here, above = split(dot(window, w1[...]), c1)
        for col in range(lo, hi):
            a = slice((col - lo) * both, (col - lo) * both + frames)
            b = slice((col - lo) * both + frames, (col - lo + 1) * both)
            rows = slice(col * frames, (col + 1) * frames)
            p_up[rows] = above[a].astype(BF16)
            p_down[rows] = below[b].astype(BF16)
            acc[0, rows] = here[a] + above[b]
            acc[1, rows] = here[b] + below[a]
        start(has_up, first_up[c])
        start(has_down, first_down[c])

    def convolve_second(c):
        received(has_down, first_up[c])
        received(has_up, first_down[c])
        for r, came in ((0, r_up), (1, r_down)):
            for col in range(edges[c], edges[c + 1]):
                rows = slice(col * frames, (col + 1) * frames)
                h = jnp.maximum(acc[r, rows] + came[rows].astype(F32) + b1_ref[...], 0.0)
                hid[r, :, (col + 1) * c1 : (col + 2) * c1] = h.astype(BF16)
        lo, hi = packs[c], packs[c + 1]
        window = jnp.concatenate(
            [
                hid[r, :, g * GROUP * c1 : g * GROUP * c1 + span]
                for r in range(2)
                for g in range(lo, hi)
            ],
            axis=0,
        )
        below, here, above = split(dot_t(window, w2[...]), GROUP * c2)
        n = (hi - lo) * frames
        rows = slice(lo * frames, hi * frames)
        s_up[rows] = above[:n].astype(BF16)
        s_down[rows] = below[n:].astype(BF16)
        acc2[0, rows] = here[:n] + above[n:]
        acc2[1, rows] = here[n:] + below[:n]
        start(has_up, second_up[c])
        start(has_down, second_down[c])

    def final(c):
        received(has_down, second_up[c])
        received(has_up, second_down[c])
        for r, came in ((0, t_up), (1, t_down)):
            for g in range(packs[c], packs[c + 1]):
                rows = slice(g * frames, (g + 1) * frames)
                out = jnp.maximum(acc2[r, rows] + came[rows].astype(F32) + b2, 0.0).astype(BF16)
                cols = min(GROUP, width - g * GROUP) * c2
                at = g * GROUP * c2
                o_ref[r, :, at : at + cols] = out[:, 0:cols]

    for c in range(chunks):
        received(has_prev, halo_copies[c])
        part = slice(bounds[c] * both, bounds[c + 1] * both)
        hkv[part] = dot(halo[part], win_ref[:, channels : 3 * channels]).astype(BF16)
        last = -(-bounds[c + 1] * 2 // UNROLL)
        lax.fori_loop(bounds[c] * 2 // UNROLL, last, step, 0)
        mixed = x_ref[part].astype(F32) + dot(att[part], wout_ref[...])
        grid_x[(bounds[c] + 1) * both : (bounds[c + 1] + 1) * both] = mixed.astype(BF16)
        convolve_first(c)
        if c > 0:
            convolve_second(c - 1)
    for c in range(chunks - 1):
        final(c)
    convolve_second(chunks - 1)
    final(chunks - 1)

    @pl.when(has_next)
    def _():
        for one in [mask_copy] + halo_copies:
            one.wait_send()

    @pl.when(has_up)
    def _():
        for one in first_up + second_up:
            one.wait_send()

    @pl.when(has_down)
    def _():
        for one in first_down + second_down:
            one.wait_send()


def body(
    n_row,
    n_tm,
    features,
    frame_mask,
    norm_gain,
    input_weight,
    output_weight,
    first_kernel,
    first_bias,
    second_kernel,
    second_bias,
):
    frames, rows, width, channels = features.shape
    assert frames == WIN and rows == 2
    places = rows * width
    tokens = places * frames
    padded = -(-places // UNROLL) * UNROLL * frames
    c1 = first_kernel.shape[2]
    c2 = second_kernel.shape[2]
    groups = (width + GROUP - 1) // GROUP
    x = features.transpose(2, 1, 0, 3).reshape(tokens, channels)
    even = UNROLL // 2
    piece = even * -(-width // (even * CHUNKS))
    bounds = tuple(range(0, width, piece)) + (width,)
    slots = 5 * (len(bounds) - 1) + 1
    vmem = pltpu.VMEM
    out = pl.pallas_call(
        functools.partial(kernel, width, bounds, n_row, n_tm),
        out_shape=jax.ShapeDtypeStruct((rows, frames, width * c2), BF16),
        in_specs=[pl.BlockSpec(memory_space=pltpu.VMEM)] * 9,
        out_specs=pl.BlockSpec(memory_space=pltpu.VMEM),
        scratch_shapes=[
            vmem((tokens, channels), BF16),
            vmem((tokens, channels), BF16),
            vmem((1, frames), jnp.int32),
            vmem((padded, 3 * channels), BF16),
            vmem((padded, 2 * channels), BF16),
            vmem((padded, channels), BF16),
            vmem((HEADS * frames, channels), BF16),
            vmem((frames, HEADS * frames), F32),
            vmem(((width + 2) * rows * frames, channels), BF16),
            vmem((TAPS * channels, TAPS * c1), BF16),
            vmem((TAPS * GROUP * c2, (GROUP + TAPS - 1) * c1), BF16),
            vmem((rows, width * frames, c1), F32),
            vmem((width * frames, c1), BF16),
            vmem((width * frames, c1), BF16),
            vmem((width * frames, c1), BF16),
            vmem((width * frames, c1), BF16),
            vmem((rows, frames, (groups * GROUP + TAPS - 1) * c1), BF16),
            vmem((rows, groups * frames, GROUP * c2), F32),
            vmem((groups * frames, GROUP * c2), BF16),
            vmem((groups * frames, GROUP * c2), BF16),
            vmem((groups * frames, GROUP * c2), BF16),
            vmem((groups * frames, GROUP * c2), BF16),
            pltpu.SemaphoreType.DMA((slots,)),
            pltpu.SemaphoreType.DMA((slots,)),
        ],
        compiler_params=pltpu.CompilerParams(
            collective_id=0, has_side_effects=True, vmem_limit_bytes=30 * 1024 * 1024
        ),
    )(
        x,
        frame_mask[None],
        norm_gain[None],
        input_weight,
        output_weight,
        first_kernel,
        first_bias[None],
        second_kernel.transpose(0, 2, 1),
        second_bias[None],
    )
    return out.transpose(1, 0, 2)


def solution(mesh):
    placed = (P("row", "tm", None, None), P("row"), P(), P(), P(), P(), P(), P(), P())
    return jax.shard_map(
        functools.partial(body, mesh.shape["row"], mesh.shape["tm"]),
        mesh=mesh,
        in_specs=placed,
        out_specs=P("row", "tm", None),
        check_vma=False,
    )
```

time: 59.5 us -> 35.6 us (0.60)
  the two profiles are of different devices: /device:TPU:0 before, /device:TPU:4 now
where the time goes in v2:
time: 35.6 us; the launch traced here: 35.5 us
  Pallas kernels  32.9 us (92%)
  local copies, waits for them, and re-layouts  2.47 us (7%)
    pallas_call x1, Pallas kernels, body(): pl.pallas_call(functools.partial(kernel, width, bounds, n_row, n_tm), out...  32.9 us
    transpose x1, local copies, waits for them, and re-layouts, body(): x = features.transpose(2, 1, 0, 3).reshape(tokens, channels)  1.6 us
    transpose x1, local copies, waits for them, and re-layouts, body(): return out.transpose(1, 0, 2)  0.84 us

profile of v2, /device:TPU:4, one launch (start us, length us, event | category | flops | bytes accessed | tf_op | source)
XLA Modules:
  0.0 35.5 jit_solution(15953668003977066859)
XLA Ops:
  0.0 0.0 copy-start
  0.0 0.0 copy-start.1
  0.0 0.0 copy-start.2
  0.0 0.0 copy-start.3
  0.0 0.0 copy-start.4
  0.0 0.0 copy-start.5
  0.0 0.0 copy-start.6
  0.0 0.0 copy-start.7
  0.1 1.6 %copy.10 = bf16[37,2,32,256]{3,2,1,0:T(8,128)(2,1)S(1)} copy(bf16[37,2,32,256]{3,1,0,2:T(2,128)(2,1)} %bitcast.15) | data formatting | bytes 2424832 | tf_op jit(solution)/shard_map/transpose | solution.py:367
  1.7 0.0 copy-done
  1.7 0.0 copy-done.1
  1.7 0.0 copy-done.2
  1.7 0.0 copy-done.3
  1.7 0.0 copy-done.4
  1.7 0.0 copy-done.5
  1.7 0.0 copy-done.6
  1.7 0.0 copy-done.7
  1.8 32.9 %shard_map.91 = bf16[2,32,1184]{2,1,0:T(8,128)(2,1)S(1)} custom-call(bf16[2368,256]{1,0:T(8,128)(2,1)S(1)} %bitcast.8, s32[1,32]{1,0:T(1,128)S(1)} %bitcast.12, f32[1,256]{1,0:T(1,128)S(1)} %bitcast.11, bf16[256,768]{1,0:T(8,128)(2,1)S(1)} %copy-done.1, bf16[256,256]{1,0:T(8,128)(2,1)S(1)} %copy-done.2, bf16[9,256,128]{2,1,0:T(8,128)(2,1)S(1)} %copy-done, ...), custom_call_target="tpu_custom_call" | custom-call | tf_op jit(solution)/shard_map/pallas_call | solution.py:373
  34.7 0.8 %copy.11 = bf16[32,2,1184]{2,1,0:T(2,128)(2,1)} copy(bf16[32,2,1184]{2,0,1:T(8,128)(2,1)S(1)} %bitcast.9) | data formatting | bytes 303104 | tf_op jit(solution)/shard_map/transpose | solution.py:418
Async XLA Ops:
  0.0 1.7 %copy-start = (bf16[9,256,128]{2,1,0:T(8,128)(2,1)S(1)}, bf16[9,256,128]{2,1,0:T(8,128)(2,1)}, u32[]{:S(2)}) copy-start(bf16[9,256,128]{2,1,0:T(8,128)(2,1)} %k1_ref.1) | copy-start | bytes 1769476
  0.0 1.7 %copy-start.1 = (bf16[256,768]{1,0:T(8,128)(2,1)S(1)}, bf16[256,768]{1,0:T(8,128)(2,1)}, u32[]{:S(2)}) copy-start(bf16[256,768]{1,0:T(8,128)(2,1)} %win_ref.1) | copy-start | bytes 1179652
  0.0 1.7 %copy-start.2 = (bf16[256,256]{1,0:T(8,128)(2,1)S(1)}, bf16[256,256]{1,0:T(8,128)(2,1)}, u32[]{:S(2)}) copy-start(bf16[256,256]{1,0:T(8,128)(2,1)} %wout_ref.1) | copy-start | bytes 393220
  0.0 1.7 %copy-start.3 = (bf16[9,128,32]{1,2,0:T(8,128)(2,1)S(1)}, bf16[9,128,32]{1,2,0:T(8,128)(2,1)}, u32[]{:S(2)}) copy-start(bf16[9,128,32]{1,2,0:T(8,128)(2,1)} %param.16) | copy-start | bytes 221188
  0.0 1.7 %copy-start.4 = (f32[256]{0:T(256)S(1)}, f32[256]{0:T(256)}, u32[]{:S(2)}) copy-start(f32[256]{0:T(256)} %param.11) | copy-start | bytes 3076
  0.0 1.7 %copy-start.5 = (s32[32]{0:T(128)S(1)}, s32[32]{0:T(128)}, u32[]{:S(2)}) copy-start(s32[32]{0:T(128)} %param.10) | copy-start | bytes 388
  0.0 1.7 %copy-start.6 = (f32[128]{0:T(128)S(1)}, f32[128]{0:T(128)}, u32[]{:S(2)}) copy-start(f32[128]{0:T(128)} %param.15) | copy-start | bytes 1540
  0.0 1.7 %copy-start.7 = (f32[32]{0:T(128)S(1)}, f32[32]{0:T(128)}, u32[]{:S(2)}) copy-start(f32[32]{0:T(128)} %param.17) | copy-start | bytes 388

commit v3 on v2

--- a/solution.py
+++ b/solution.py
@@ -13,7 +13,7 @@
 TAPS = 3
 GROUP = 4
 UNROLL = 4
-CHUNKS = 4
+CUTS = (0.22, 0.48, 0.76, 0.92)
 NEG = -1e30
 epsilon = 1e-05
 MESH = pl.DeviceIdType.MESH
@@ -320,12 +320,12 @@
         mixed = x_ref[part].astype(F32) + dot(att[part], wout_ref[...])
         grid_x[(bounds[c] + 1) * both : (bounds[c + 1] + 1) * both] = mixed.astype(BF16)
         convolve_first(c)
-        if c > 0:
-            convolve_second(c - 1)
-    for c in range(chunks - 1):
+        if c >= 2:
+            convolve_second(c - 2)
+    for c in range(chunks - 2, chunks):
+        convolve_second(c)
+    for c in range(chunks):
         final(c)
-    convolve_second(chunks - 1)
-    final(chunks - 1)
 
     @pl.when(has_next)
     def _():
@@ -366,8 +366,7 @@
     groups = (width + GROUP - 1) // GROUP
     x = features.transpose(2, 1, 0, 3).reshape(tokens, channels)
     even = UNROLL // 2
-    piece = even * -(-width // (even * CHUNKS))
-    bounds = tuple(range(0, width, piece)) + (width,)
+    bounds = (0,) + tuple(even * round(width * cut / even) for cut in CUTS) + (width,)
     slots = 5 * (len(bounds) - 1) + 1
     vmem = pltpu.VMEM
     out = pl.pallas_call(

time: 35.6 us -> 34.2 us (0.961)
  Pallas kernels: 32.9 us -> 31.5 us
    pallas_call x1, Pallas kernels: 32.9 us -> 31.5 us  [body(): pl.pallas_call(functools.partial(kernel, width, bounds, n_row, n_tm), out...]
where the time goes in v3:
time: 34.2 us; the launch traced here: 34.1 us
  Pallas kernels  31.5 us (92%)
  local copies, waits for them, and re-layouts  2.47 us (7%)
    pallas_call x1, Pallas kernels, body(): pl.pallas_call(functools.partial(kernel, width, bounds, n_row, n_tm), out...  31.5 us
    transpose x1, local copies, waits for them, and re-layouts, body(): x = features.transpose(2, 1, 0, 3).reshape(tokens, channels)  1.6 us
    transpose x1, local copies, waits for them, and re-layouts, body(): return out.transpose(1, 0, 2)  0.84 us

profile of v3, /device:TPU:4, one launch (start us, length us, event | category | flops | bytes accessed | tf_op | source)
XLA Modules:
  0.0 34.1 jit_solution(14657575969811352982)
XLA Ops:
  0.0 0.0 copy-start
  0.0 0.0 copy-start.1
  0.0 0.0 copy-start.2
  0.0 0.0 copy-start.3
  0.0 0.0 copy-start.4
  0.0 0.0 copy-start.5
  0.0 0.0 copy-start.6
  0.0 0.0 copy-start.7
  0.1 1.6 %copy.10 = bf16[37,2,32,256]{3,2,1,0:T(8,128)(2,1)S(1)} copy(bf16[37,2,32,256]{3,1,0,2:T(2,128)(2,1)} %bitcast.15) | data formatting | bytes 2424832 | tf_op jit(solution)/shard_map/transpose | solution.py:367
  1.7 0.0 copy-done
  1.7 0.0 copy-done.1
  1.7 0.0 copy-done.2
  1.7 0.0 copy-done.3
  1.7 0.0 copy-done.4
  1.7 0.0 copy-done.5
  1.7 0.0 copy-done.6
  1.7 0.0 copy-done.7
  1.8 31.5 %shard_map.91 = bf16[2,32,1184]{2,1,0:T(8,128)(2,1)S(1)} custom-call(bf16[2368,256]{1,0:T(8,128)(2,1)S(1)} %bitcast.8, s32[1,32]{1,0:T(1,128)S(1)} %bitcast.12, f32[1,256]{1,0:T(1,128)S(1)} %bitcast.11, bf16[256,768]{1,0:T(8,128)(2,1)S(1)} %copy-done.1, bf16[256,256]{1,0:T(8,128)(2,1)S(1)} %copy-done.2, bf16[9,256,128]{2,1,0:T(8,128)(2,1)S(1)} %copy-done, ...), custom_call_target="tpu_custom_call" | custom-call | tf_op jit(solution)/shard_map/pallas_call | solution.py:372
  33.2 0.8 %copy.11 = bf16[32,2,1184]{2,1,0:T(2,128)(2,1)} copy(bf16[32,2,1184]{2,0,1:T(8,128)(2,1)S(1)} %bitcast.9) | data formatting | bytes 303104 | tf_op jit(solution)/shard_map/transpose | solution.py:417
Async XLA Ops:
  0.0 1.7 %copy-start = (bf16[9,256,128]{2,1,0:T(8,128)(2,1)S(1)}, bf16[9,256,128]{2,1,0:T(8,128)(2,1)}, u32[]{:S(2)}) copy-start(bf16[9,256,128]{2,1,0:T(8,128)(2,1)} %k1_ref.1) | copy-start | bytes 1769476
  0.0 1.7 %copy-start.1 = (bf16[256,768]{1,0:T(8,128)(2,1)S(1)}, bf16[256,768]{1,0:T(8,128)(2,1)}, u32[]{:S(2)}) copy-start(bf16[256,768]{1,0:T(8,128)(2,1)} %win_ref.1) | copy-start | bytes 1179652
  0.0 1.7 %copy-start.2 = (bf16[256,256]{1,0:T(8,128)(2,1)S(1)}, bf16[256,256]{1,0:T(8,128)(2,1)}, u32[]{:S(2)}) copy-start(bf16[256,256]{1,0:T(8,128)(2,1)} %wout_ref.1) | copy-start | bytes 393220
  0.0 1.7 %copy-start.3 = (bf16[9,128,32]{1,2,0:T(8,128)(2,1)S(1)}, bf16[9,128,32]{1,2,0:T(8,128)(2,1)}, u32[]{:S(2)}) copy-start(bf16[9,128,32]{1,2,0:T(8,128)(2,1)} %param.16) | copy-start | bytes 221188
  0.0 1.7 %copy-start.4 = (f32[256]{0:T(256)S(1)}, f32[256]{0:T(256)}, u32[]{:S(2)}) copy-start(f32[256]{0:T(256)} %param.11) | copy-start | bytes 3076
  0.0 1.7 %copy-start.5 = (s32[32]{0:T(128)S(1)}, s32[32]{0:T(128)}, u32[]{:S(2)}) copy-start(s32[32]{0:T(128)} %param.10) | copy-start | bytes 388
  0.0 1.7 %copy-start.6 = (f32[128]{0:T(128)S(1)}, f32[128]{0:T(128)}, u32[]{:S(2)}) copy-start(f32[128]{0:T(128)} %param.15) | copy-start | bytes 1540
  0.0 1.7 %copy-start.7 = (f32[32]{0:T(128)S(1)}, f32[32]{0:T(128)}, u32[]{:S(2)}) copy-start(f32[32]{0:T(128)} %param.17) | copy-start | bytes 388
